TPU v7x, 32 devices: a whole 2x2x4 slice. The times are simulated.
32 devices in a mesh: dp: 8 (over z, x), tensor: 4 (over y, core).
Axes of the slice: x: 2, y: 2, z: 4, core: 2. Of those that a mesh axis runs over, the one named last changes fastest.
Arguments:
- hidden_in: float32 [4096, 1536], P('dp'), may hold values from -6 to 6
- doc_lengths: int32 [2, 2], replicated, may hold values from 1 to 1792, 2048 in all within a row
- norm_attn: float32 [2, 1536], replicated, may hold values from 0.5 to 1.5
- norm_mlp: float32 [2, 1536], replicated, may hold values from 0.5 to 1.5
- w_query: bfloat16 [2, 1536, 1536], P(None, None, 'tensor'), may hold values from -0.15625 to 0.15625
- w_key: bfloat16 [2, 1536, 768], P(None, None, 'tensor'), may hold values from -0.15625 to 0.15625
- w_value: bfloat16 [2, 1536, 768], P(None, None, 'tensor'), may hold values from -0.15625 to 0.15625
- w_out: bfloat16 [2, 1536, 1536], P(None, 'tensor'), may hold values from -0.625 to 0.625
- w_gate: bfloat16 [2, 1536, 4096], P(None, None, 'tensor'), may hold values from -0.15625 to 0.15625
- w_up: bfloat16 [2, 1536, 4096], P(None, None, 'tensor'), may hold values from -0.15625 to 0.15625
- w_down: bfloat16 [2, 4096, 1536], P(None, 'tensor'), may hold values from -0.09375 to 0.09375
- cotangent: float32 [4096, 1536], P('dp'), may hold values from -6 to 6
Outputs:
- hidden_out: float32 [4096, 1536], P('dp')
- input_grad: float32 [4096, 1536], P('dp')
- norm_attn_grad: float32 [2, 1536], P(None, 'dp')
- norm_mlp_grad: float32 [2, 1536], P(None, 'dp')
- w_query_grad: float32 [2, 1536, 1536], P(None, 'dp', 'tensor')
- w_key_grad: float32 [2, 1536, 768], P(None, 'dp', 'tensor')
- w_value_grad: float32 [2, 1536, 768], P(None, 'dp', 'tensor')
- w_out_grad: float32 [2, 1536, 1536], P(None, 'tensor', 'dp')
- w_gate_grad: float32 [2, 1536, 4096], P(None, 'dp', 'tensor')
- w_up_grad: float32 [2, 1536, 4096], P(None, 'dp', 'tensor')
- w_down_grad: float32 [2, 4096, 1536], P(None, 'tensor', 'dp')
Inputs may be any that keep to these rules, and one draw needn't show every extreme that they name: `doc_lengths`: each row holds 2 document lengths that add up to 2048, each at most 1792.
All inputs are finite; a program needn't handle non-finite values.
Results may differ from a plain program's by a relative error of at most 0.028.
Values may be sent and summed in bfloat16 or wider, within the bound.
No kernel may reach another device: no remote copies, remote signals or barrier semaphores. Data moves between devices by JAX's collectives and lax.ppermute only.
A program may use at most 320 MiB of HBM per device.

v0:
```python
import jax
import jax.numpy as jnp
from jax import lax
from jax.sharding import PartitionSpec as P

HD = 96
LAYERS = 2
STRETCHES = 4
EPS = 1e-05
BASE = 100000.0


def passed_along(block, axis, distance):
    devices = range(lax.axis_size(axis))
    route = [((i - distance) % len(devices), i) for i in devices]
    return lax.ppermute(block, axis, route)


def rope_tables(positions):
    half_dim = HD // 2
    frequency = BASE ** (-(jnp.arange(half_dim, dtype=jnp.float32) * 2.0 / HD))
    angles = positions.astype(jnp.float32)[:, None] * frequency[None, :]
    angles = jnp.concatenate([angles, angles], axis=1)
    return (jnp.cos(angles)[:, None, :], jnp.sin(angles)[:, None, :])


def rotate(values, cosine, sine_table):
    half_dim = values.shape[-1] // 2
    turned = jnp.concatenate([-values[..., half_dim:], values[..., :half_dim]], axis=-1)
    return values * cosine + turned * sine_table


def unrotate(gradient, cosine, sine_table):
    half_dim = gradient.shape[-1] // 2
    scaled_values = gradient * sine_table
    turned = jnp.concatenate(
        [scaled_values[..., half_dim:], -scaled_values[..., :half_dim]], axis=-1
    )
    return gradient * cosine + turned


def doc_place(places, lengths):
    doc_ends = jnp.cumsum(lengths, axis=1)
    passed = (places[:, None] >= doc_ends).astype(jnp.int32)
    doc_ids = jnp.sum(passed, axis=1)
    starts = jnp.sum(passed * lengths, axis=1)
    return (doc_ids, places - starts)


def scores_of(queries, key_rows, allowed):
    scores = jnp.einsum(
        "qkgd,tkd->kgqt", queries, key_rows, preferred_element_type=jnp.float32
    ) * HD ** (-0.5)
    return jnp.where(allowed[None, None], scores, -jnp.inf)


def attention_forward(queries, key_rows, value_rows, allowed):
    scores = scores_of(queries, key_rows, allowed)
    row_top = jnp.max(scores, axis=-1, keepdims=True)
    log_total = row_top + jnp.log(jnp.sum(jnp.exp(scores - row_top), axis=-1, keepdims=True))
    attn_probs = jnp.exp(scores - log_total).astype(jnp.bfloat16)
    mixed_heads = jnp.einsum(
        "kgqt,tkd->qkgd", attn_probs, value_rows, preferred_element_type=jnp.float32
    )
    return (mixed_heads.astype(jnp.bfloat16), log_total)


def attention_backward(queries, key_rows, value_rows, allowed, log_total, mixed_grad):
    scores = scores_of(queries, key_rows, allowed)
    attn_probs = jnp.exp(scores - log_total)
    prob_grad = jnp.einsum(
        "qkgd,tkd->kgqt", mixed_grad, value_rows, preferred_element_type=jnp.float32
    )
    centre = jnp.sum(attn_probs * prob_grad, axis=-1, keepdims=True)
    score_grad = (attn_probs * (prob_grad - centre) * HD ** (-0.5)).astype(jnp.bfloat16)
    probs_bf = attn_probs.astype(jnp.bfloat16)
    value_grad = jnp.einsum(
        "kgqt,qkgd->tkd", probs_bf, mixed_grad, preferred_element_type=jnp.float32
    )
    query_grad = jnp.einsum(
        "kgqt,tkd->qkgd", score_grad, key_rows, preferred_element_type=jnp.float32
    )
    key_grad = jnp.einsum("kgqt,qkgd->tkd", score_grad, queries, preferred_element_type=jnp.float32)
    return (query_grad, key_grad, value_grad)


def norm_back(residual_stream, inverse_norm, gain, normalized_gradient, incoming_gradient):
    normalized_input = residual_stream * inverse_norm
    scaled_values = normalized_gradient * gain
    gain_gradient = jnp.sum(normalized_gradient * normalized_input, axis=0)
    residual_gradient = incoming_gradient + inverse_norm * (
        scaled_values
        - normalized_input * jnp.mean(scaled_values * normalized_input, axis=1, keepdims=True)
    )
    return (residual_gradient, gain_gradient)


def forward_layer(residual_stream, params, tables, allowed):
    gain_attn, gain_mlp, query_w, key_w, value_w, out_w, gate_w, up_w, down_w = params
    cosine, sine_table = tables
    row_count = residual_stream.shape[0]
    query_heads = query_w.shape[1] // HD
    kv_heads = key_w.shape[1] // HD
    inv_attn = lax.rsqrt(jnp.mean(residual_stream * residual_stream, axis=1, keepdims=True) + EPS)
    normed_attn = (residual_stream * inv_attn * gain_attn).astype(jnp.bfloat16)
    queries = jnp.dot(normed_attn, query_w, preferred_element_type=jnp.float32).reshape(
        row_count, query_heads, HD
    )
    queries = rotate(queries, cosine, sine_table).astype(jnp.bfloat16)
    key_rows = jnp.dot(normed_attn, key_w, preferred_element_type=jnp.float32).reshape(
        row_count, kv_heads, HD
    )
    key_rows = (
        rotate(key_rows, cosine, sine_table).astype(jnp.bfloat16).reshape(row_count, kv_heads * HD)
    )
    value_rows = jnp.dot(normed_attn, value_w, preferred_element_type=jnp.float32).astype(
        jnp.bfloat16
    )
    key_list = [key_rows]
    value_list = [value_rows]
    for distance in range(1, STRETCHES):
        moved_keys, moved_values = passed_along((key_rows, value_rows), "dp", distance)
        key_list.append(moved_keys)
        value_list.append(moved_values)
    all_keys = jnp.concatenate(key_list, axis=0).reshape(STRETCHES * row_count, kv_heads, HD)
    all_values = jnp.concatenate(value_list, axis=0).reshape(STRETCHES * row_count, kv_heads, HD)
    grouped = queries.reshape(row_count, kv_heads, query_heads // kv_heads, HD)
    mixed_heads, log_total = attention_forward(grouped, all_keys, all_values, allowed)
    mixed_heads = mixed_heads.reshape(row_count, query_heads * HD)
    head_part = jnp.dot(mixed_heads, out_w, preferred_element_type=jnp.float32)
    middle = residual_stream + lax.psum(head_part, "tensor")
    inv_mlp = lax.rsqrt(jnp.mean(middle * middle, axis=1, keepdims=True) + EPS)
    normed_mlp = (middle * inv_mlp * gain_mlp).astype(jnp.bfloat16)
    gate_pre = jnp.dot(normed_mlp, gate_w, preferred_element_type=jnp.float32)
    up_values = jnp.dot(normed_mlp, up_w, preferred_element_type=jnp.float32)
    activated = (jax.nn.silu(gate_pre) * up_values).astype(jnp.bfloat16)
    unit_part = jnp.dot(activated, down_w, preferred_element_type=jnp.float32)
    result = middle + lax.psum(unit_part, "tensor")
    record = (
        residual_stream,
        inv_attn,
        normed_attn,
        grouped,
        all_keys,
        all_values,
        log_total,
        mixed_heads,
        middle,
        inv_mlp,
        normed_mlp,
        gate_pre,
        up_values,
        activated,
    )
    return (record, result)


def backward_layer(grad_flow, record, params, tables, allowed):
    gain_attn, gain_mlp, query_w, key_w, value_w, out_w, gate_w, up_w, down_w = params
    (
        residual_stream,
        inv_attn,
        normed_attn,
        grouped,
        all_keys,
        all_values,
        log_total,
        mixed_heads,
        middle,
        inv_mlp,
        normed_mlp,
        gate_pre,
        up_values,
        activated,
    ) = record
    cosine, sine_table = tables
    row_count = residual_stream.shape[0]
    query_heads = query_w.shape[1] // HD
    kv_heads = key_w.shape[1] // HD
    down_in = grad_flow.astype(jnp.bfloat16)
    grad_down = jnp.dot(activated.T, down_in, preferred_element_type=jnp.float32)
    hidden_grad = jnp.dot(down_in, down_w.T, preferred_element_type=jnp.float32)
    sigmoid_gate = jax.nn.sigmoid(gate_pre)
    gate_grad = (
        hidden_grad * up_values * sigmoid_gate * (1.0 + gate_pre * (1.0 - sigmoid_gate))
    ).astype(jnp.bfloat16)
    up_grad = (hidden_grad * gate_pre * sigmoid_gate).astype(jnp.bfloat16)
    grad_gate = jnp.dot(normed_mlp.T, gate_grad, preferred_element_type=jnp.float32)
    grad_up = jnp.dot(normed_mlp.T, up_grad, preferred_element_type=jnp.float32)
    unit_back = jnp.dot(gate_grad, gate_w.T, preferred_element_type=jnp.float32) + jnp.dot(
        up_grad, up_w.T, preferred_element_type=jnp.float32
    )
    mlp_norm_grad = lax.psum(unit_back, "tensor")
    middle_grad, grad_gain_mlp = norm_back(middle, inv_mlp, gain_mlp, mlp_norm_grad, grad_flow)
    out_in = middle_grad.astype(jnp.bfloat16)
    grad_out = jnp.dot(mixed_heads.T, out_in, preferred_element_type=jnp.float32)
    mixed_grad = jnp.dot(out_in, out_w.T, preferred_element_type=jnp.float32).astype(jnp.bfloat16)
    mixed_grad = mixed_grad.reshape(row_count, kv_heads, query_heads // kv_heads, HD)
    query_grad, key_grad, value_grad = attention_backward(
        grouped, all_keys, all_values, allowed, log_total, mixed_grad
    )
    key_grad = key_grad.reshape(STRETCHES * row_count, kv_heads * HD)
    value_grad = value_grad.reshape(STRETCHES * row_count, kv_heads * HD)
    key_total = key_grad[:row_count]
    value_total = value_grad[:row_count]
    for distance in range(1, STRETCHES):
        key_piece = key_grad[distance * row_count : (distance + 1) * row_count]
        value_piece = value_grad[distance * row_count : (distance + 1) * row_count]
        moved_keys, moved_values = passed_along((key_piece, value_piece), "dp", -distance)
        key_total = key_total + moved_keys
        value_total = value_total + moved_values
    query_grad = (
        unrotate(query_grad.reshape(row_count, query_heads, HD), cosine, sine_table)
        .astype(jnp.bfloat16)
        .reshape(row_count, query_heads * HD)
    )
    key_total = (
        unrotate(key_total.reshape(row_count, kv_heads, HD), cosine, sine_table)
        .astype(jnp.bfloat16)
        .reshape(row_count, kv_heads * HD)
    )
    value_total = value_total.astype(jnp.bfloat16)
    grad_query = jnp.dot(normed_attn.T, query_grad, preferred_element_type=jnp.float32)
    grad_key = jnp.dot(normed_attn.T, key_total, preferred_element_type=jnp.float32)
    grad_value = jnp.dot(normed_attn.T, value_total, preferred_element_type=jnp.float32)
    head_back = jnp.dot(query_grad, query_w.T, preferred_element_type=jnp.float32)
    head_back = head_back + jnp.dot(key_total, key_w.T, preferred_element_type=jnp.float32)
    head_back = head_back + jnp.dot(value_total, value_w.T, preferred_element_type=jnp.float32)
    attn_norm_grad = lax.psum(head_back, "tensor")
    residual_gradient, grad_gain_attn = norm_back(
        residual_stream, inv_attn, gain_attn, attn_norm_grad, middle_grad
    )
    return (
        residual_gradient,
        (
            grad_gain_attn,
            grad_gain_mlp,
            grad_query,
            grad_key,
            grad_value,
            grad_out,
            grad_gate,
            grad_up,
            grad_down,
        ),
    )


def shards(
    hidden_in,
    doc_lengths,
    norm_attn,
    norm_mlp,
    w_query,
    w_key,
    w_value,
    w_out,
    w_gate,
    w_up,
    w_down,
    cotangent,
):
    row_count = hidden_in.shape[0]
    seq_count = lax.axis_size("dp") // STRETCHES
    shifted_index = lax.axis_index("dp") + STRETCHES // 2
    stretch_index = shifted_index % STRETCHES
    seq_index = shifted_index // STRETCHES % seq_count
    lengths = lax.dynamic_slice_in_dim(doc_lengths, seq_index, 1, 0)
    local_rows = jnp.arange(row_count, dtype=jnp.int32)
    query_place = stretch_index * row_count + local_rows
    query_doc, query_pos = doc_place(query_place, lengths)
    key_parts = []
    for distance in range(STRETCHES):
        key_parts.append((stretch_index - distance) * row_count + local_rows)
    key_place = jnp.concatenate(key_parts)
    key_doc = doc_place(key_place, lengths)[0]
    allowed = (
        (key_place[None, :] >= 0)
        & (key_place[None, :] <= query_place[:, None])
        & (key_doc[None, :] == query_doc[:, None])
    )
    tables = rope_tables(query_pos)
    records = []
    flowing = hidden_in
    for layer_index in range(LAYERS):
        params = (
            norm_attn[layer_index],
            norm_mlp[layer_index],
            w_query[layer_index],
            w_key[layer_index],
            w_value[layer_index],
            w_out[layer_index],
            w_gate[layer_index],
            w_up[layer_index],
            w_down[layer_index],
        )
        record, flowing = forward_layer(flowing, params, tables, allowed)
        records.append(record)
    grad_flow = cotangent
    collected = [None] * LAYERS
    for layer_index in reversed(range(LAYERS)):
        params = (
            norm_attn[layer_index],
            norm_mlp[layer_index],
            w_query[layer_index],
            w_key[layer_index],
            w_value[layer_index],
            w_out[layer_index],
            w_gate[layer_index],
            w_up[layer_index],
            w_down[layer_index],
        )
        grad_flow, layer_grads = backward_layer(
            grad_flow, records[layer_index], params, tables, allowed
        )
        collected[layer_index] = layer_grads
    stacked = tuple(
        (jnp.stack([member[position] for member in collected]) for position in range(9))
    )
    stacked = (
        lax.psum_scatter(
            stacked[0].astype(jnp.bfloat16), "dp", scatter_dimension=1, tiled=True
        ).astype(jnp.float32),
        lax.psum_scatter(
            stacked[1].astype(jnp.bfloat16), "dp", scatter_dimension=1, tiled=True
        ).astype(jnp.float32),
        lax.psum_scatter(
            stacked[2].astype(jnp.bfloat16), "dp", scatter_dimension=1, tiled=True
        ).astype(jnp.float32),
        lax.psum_scatter(
            stacked[3].astype(jnp.bfloat16), "dp", scatter_dimension=1, tiled=True
        ).astype(jnp.float32),
        lax.psum_scatter(
            stacked[4].astype(jnp.bfloat16), "dp", scatter_dimension=1, tiled=True
        ).astype(jnp.float32),
        lax.psum_scatter(
            stacked[5].astype(jnp.bfloat16), "dp", scatter_dimension=2, tiled=True
        ).astype(jnp.float32),
        lax.psum_scatter(
            stacked[6].astype(jnp.bfloat16), "dp", scatter_dimension=1, tiled=True
        ).astype(jnp.float32),
        lax.psum_scatter(
            stacked[7].astype(jnp.bfloat16), "dp", scatter_dimension=1, tiled=True
        ).astype(jnp.float32),
        lax.psum_scatter(
            stacked[8].astype(jnp.bfloat16), "dp", scatter_dimension=2, tiled=True
        ).astype(jnp.float32),
    )
    return (
        flowing,
        grad_flow,
        stacked[0],
        stacked[1],
        stacked[2],
        stacked[3],
        stacked[4],
        stacked[5],
        stacked[6],
        stacked[7],
        stacked[8],
    )


def solution(mesh):
    placed = (
        P("dp", None),
        P(),
        P(),
        P(),
        P(None, None, "tensor"),
        P(None, None, "tensor"),
        P(None, None, "tensor"),
        P(None, "tensor", None),
        P(None, None, "tensor"),
        P(None, None, "tensor"),
        P(None, "tensor", None),
        P("dp", None),
    )
    return jax.shard_map(
        shards,
        mesh=mesh,
        in_specs=placed,
        out_specs=(
            P("dp", None),
            P("dp", None),
            P(None, "dp"),
            P(None, "dp"),
            P(None, "dp", "tensor"),
            P(None, "dp", "tensor"),
            P(None, "dp", "tensor"),
            P(None, "tensor", "dp"),
            P(None, "dp", "tensor"),
            P(None, "dp", "tensor"),
            P(None, "tensor", "dp"),
        ),
        check_vma=False,
    )
```

profile of v0, /device:TPU:0, one launch (start us, length us, event | category | flops | bytes accessed | tf_op | source)
XLA Modules:
  0.0 1885.0 jit_solution(11726850413629536480)
XLA Ops:
  38.5 14.9 collective-permute-done.5
  72.2 64.6 %all-reduce.13.cloned.1.call-done = f32[512,1536]{1,0:T(8,128)} async-done(((f32[512,1536]{1,0:T(8,128)}), f32[512,1536]{1,0:T(8,128)}) %all-reduce.13.cloned.1.call-update) | async-done | bytes 3145744 | tf_op jit(solution)/shard_map/psum | solution.py:131
  155.3 66.3 %all-reduce.15.cloned.1.call-done = f32[512,1536]{1,0:T(8,128)} async-done(((f32[512,1536]{1,0:T(8,128)}), f32[512,1536]{1,0:T(8,128)}) %all-reduce.15.cloned.1.call-update) | async-done | bytes 3145744 | tf_op jit(solution)/shard_map/psum | solution.py:138
  238.2 22.7 %collective-permute-done.11 = bf16[512,192]{0,1:T(8,128)(2,1)S(1)} collective-permute-done((bf16[512,192]{0,1:T(8,128)(2,1)S(1)}, bf16[512,192]{0,1:T(8,128)(2,1)S(1)}, u32[]{:S(2)}, u32[]{:S(2)}) %collective-permute-start.11) | collective-permute-done | bytes 196640 | tf_op jit(solution)/shard_map/ppermute | solution.py:16
  279.3 64.6 %all-reduce.17.cloned.1.call-done = f32[512,1536]{1,0:T(8,128)} async-done(((f32[512,1536]{1,0:T(8,128)}), f32[512,1536]{1,0:T(8,128)}) %all-reduce.17.cloned.1.call-update) | async-done | bytes 3145744 | tf_op jit(solution)/shard_map/psum | solution.py:131
  365.1 68.7 %all-reduce.19.cloned.1.call-done = f32[512,1536]{1,0:T(8,128)} async-done(((f32[512,1536]{1,0:T(8,128)}), f32[512,1536]{1,0:T(8,128)}) %all-reduce.19.cloned.1.call-update) | async-done | bytes 3145744 | tf_op jit(solution)/shard_map/psum | solution.py:193
  462.0 25.3 %fusion.63 = f32[2048,2,96]{0,2,1:T(8,128)} fusion(bf16[512,2,2,96]{0,3,2,1:T(8,128)(2,1)} %bitcast.491, f32[2,2048,512,2]{2,1,3,0:T(8,128)} %fusion.188, f32[2,2048,512,2]{2,1,3,0:T(8,128)} %copy-done.12, f32[2,2,512]{2,1,0:T(2,128)} %copy-done.94, pred[512,2048]{0,1:T(8,128)(4,1)} %copy-done.25), kind=kOutput, calls=%fused_computation.113 | convolution fusion | flops 851447808 | bytes 36577280 | tf_op jit(solution)/shard_map/kgqt,qkgd->tkd/dot_general | solution.py:83
  487.3 25.1 %fusion.41 = f32[2,96,2,512]{3,1,2,0:T(8,128)} fusion(f32[2,2048,512,2]{2,1,3,0:T(8,128)} %fusion.188, f32[2,2048,512,2]{2,1,3,0:T(8,128)} %copy-done.12, f32[2,2,512]{2,1,0:T(2,128)} %copy-done.94, pred[512,2048]{0,1:T(8,128)(4,1)} %copy-done.25, bf16[512,2,96]{0,2,1:T(8,128)(2,1)} %bitcast.530, bf16[512,2,96]{0,2,1:T(8,128)(2,1)} %bitcast.528, ...), kind=kOutput, calls=%fused_computation.87 | convolution fusion | flops 854593536 | bytes 36184064 | tf_op jit(solution)/shard_map/kgqt,tkd->qkgd/dot_general | solution.py:80
  525.8 19.0 %collective-permute-done.12 = f32[512,192]{0,1:T(8,128)S(1)} collective-permute-done((f32[512,192]{0,1:T(8,128)S(1)}, f32[512,192]{0,1:T(8,128)S(1)}, u32[]{:S(2)}, u32[]{:S(2)}) %collective-permute-start.12) | collective-permute-done | bytes 393248 | tf_op jit(solution)/shard_map/ppermute | solution.py:16
  571.9 86.6 %all-reduce.21.cloned.1.call-done = f32[512,1536]{1,0:T(8,128)} async-done(((f32[512,1536]{1,0:T(8,128)}), f32[512,1536]{1,0:T(8,128)}) %all-reduce.21.cloned.1.call-update) | async-done | bytes 3145744 | tf_op jit(solution)/shard_map/psum | solution.py:229
  684.1 63.0 %all-reduce.23.cloned.1.call-done = f32[512,1536]{1,0:T(8,128)} async-done(((f32[512,1536]{1,0:T(8,128)}), f32[512,1536]{1,0:T(8,128)}) %all-reduce.23.cloned.1.call-update) | async-done | bytes 3145744 | tf_op jit(solution)/shard_map/psum | solution.py:193
  754.7 9.7 convolution_bitcast_fusion
  772.5 24.6 %fusion.62 = f32[2048,2,96]{0,2,1:T(8,128)} fusion(bf16[512,2,2,96]{0,3,2,1:T(8,128)(2,1)S(1)} %bitcast.489, f32[2,2048,512,2]{2,1,3,0:T(8,128)} %fusion.189, f32[2,2048,512,2]{2,1,3,0:T(8,128)} %copy-done.11, f32[2,2,512]{2,1,0:T(2,128)S(1)} %copy-done.93, pred[512,2048]{0,1:T(8,128)(4,1)S(1)} %copy-done.28), kind=kOutput, calls=%fused_computation.112 | convolution fusion | flops 851447808 | bytes 36577280 | tf_op jit(solution)/shard_map/kgqt,qkgd->tkd/dot_general | solution.py:83
  797.2 23.6 %fusion.44 = f32[2,96,2,512]{3,1,2,0:T(8,128)S(1)} fusion(f32[2,2048,512,2]{2,1,3,0:T(8,128)} %fusion.189, f32[2,2048,512,2]{2,1,3,0:T(8,128)} %copy-done.11, f32[2,2,512]{2,1,0:T(2,128)S(1)} %copy-done.93, pred[512,2048]{0,1:T(8,128)(4,1)S(1)} %copy-done.28, bf16[512,2,96]{0,2,1:T(8,128)(2,1)} %bitcast.14, bf16[512,2,96]{0,2,1:T(8,128)(2,1)} %bitcast.13, ...), kind=kOutput, calls=%fused_computation.90 | convolution fusion | flops 854593536 | bytes 36184064 | tf_op jit(solution)/shard_map/kgqt,tkd->qkgd/dot_general | solution.py:80
  834.4 19.0 %collective-permute-done.18 = f32[512,192]{0,1:T(8,128)S(1)} collective-permute-done((f32[512,192]{0,1:T(8,128)S(1)}, f32[512,192]{0,1:T(8,128)S(1)}, u32[]{:S(2)}, u32[]{:S(2)}) %collective-permute-start.18) | collective-permute-done | bytes 393248 | tf_op jit(solution)/shard_map/ppermute | solution.py:16
  913.4 105.2 %all-reduce.25.cloned.1.call-done = (f32[512,1536]{1,0:T(8,128)}, f32[512,1536]{1,0:T(8,128)}) async-done(((f32[512,1536]{1,0:T(8,128)}, f32[512,1536]{1,0:T(8,128)}), (f32[512,1536]{1,0:T(8,128)}, f32[512,1536]{1,0:T(8,128)})) %all-reduce.25.cloned.1.call-update) | async-done | bytes 6291472 | tf_op jit(solution)/shard_map/psum | solution.py:138
  1037.8 16.4 copy.64
  1086.7 63.9 %reduce-scatter.28.cloned.1.call-done = bf16[192,384]{1,0:T(8,128)(2,1)} async-done(((bf16[1536,384]{1,0:T(8,128)(2,1)}), bf16[192,384]{1,0:T(8,128)(2,1)}) %reduce-scatter.28.cloned.1.call-update) | async-done | bytes 147472
  1152.8 64.8 %reduce-scatter.26.cloned.1.call-done = bf16[192,384]{1,0:T(8,128)(2,1)} async-done(((bf16[1536,384]{1,0:T(8,128)(2,1)}), bf16[192,384]{1,0:T(8,128)(2,1)}) %reduce-scatter.26.cloned.1.call-update) | async-done | bytes 147472
  1227.4 54.4 %reduce-scatter.22.cloned.1.call-done = bf16[192,2]{1,0:T(8,128)(2,1)} async-done(((bf16[1536,2]{1,0:T(8,128)(2,1)}), bf16[192,2]{1,0:T(8,128)(2,1)}) %reduce-scatter.22.cloned.1.call-update) | async-done | bytes 784
  1283.3 69.9 %reduce-scatter.16.cloned.1.call-done = bf16[2,192,384]{2,1,0:T(8,128)(2,1)} async-done(((bf16[2,1536,384]{2,1,0:T(8,128)(2,1)}), bf16[2,192,384]{2,1,0:T(8,128)(2,1)}) %reduce-scatter.16.cloned.1.call-update) | async-done | bytes 294928 | tf_op jit(solution)/shard_map/reduce_scatter | solution.py:327
  1355.0 278.8 %all-reduce.27.cloned.1.call-done = (bf16[2,384,1536]{1,0,2:T(2,128)(2,1)}, bf16[2,1024,1536]{1,0,2:T(2,128)(2,1)}) async-done(((bf16[2,384,1536]{1,0,2:T(2,128)(2,1)}, bf16[2,1024,1536]{1,0,2:T(2,128)(2,1)}), (bf16[2,384,1536]{1,0,2:T(2,128)(2,1)}, bf16[2,1024,1536]{1,0,2:T(2,128)(2,1)})) %all-reduce.27.cloned.1.call-update) | async-done | bytes 8650768
  1639.1 115.5 %reduce-scatter.20.cloned.1.call-done = bf16[2,192,1024]{2,1,0:T(8,128)(2,1)} async-done(((bf16[2,1536,1024]{2,1,0:T(8,128)(2,1)}), bf16[2,192,1024]{2,1,0:T(8,128)(2,1)}) %reduce-scatter.20.cloned.1.call-update) | async-done | bytes 786448 | tf_op jit(solution)/shard_map/reduce_scatter | solution.py:342
  1757.1 118.5 %reduce-scatter.18.cloned.1.call-done = bf16[2,192,1024]{2,1,0:T(8,128)(2,1)} async-done(((bf16[2,1536,1024]{2,1,0:T(8,128)(2,1)}), bf16[2,192,1024]{2,1,0:T(8,128)(2,1)}) %reduce-scatter.18.cloned.1.call-update) | async-done | bytes 786448 | tf_op jit(solution)/shard_map/reduce_scatter | solution.py:339
  (503 shorter events, 383.2 us)
Async XLA Ops:
  7.2 129.6 %all-reduce.13.cloned.1.call-start = ((), (), s32[]{:S(2)}) async-start(), calls=%async_computation.7 | async-start | bytes 6291456 | tf_op jit(solution)/shard_map/psum | solution.py:131
  24.6 37.1 %collective-permute-start = (bf16[512,192]{0,1:T(8,128)(2,1)S(1)}, bf16[512,192]{0,1:T(8,128)(2,1)S(1)}, u32[]{:S(2)}, u32[]{:S(2)}) collective-permute-start(bf16[512,192]{0,1:T(8,128)(2,1)S(1)} %convolution_convert_fusion.19), channel_id=1, source_target_pairs={{28,0},{0,4},{4,8},{8,12},{12,16},{16,20},{20,24},{24,28},{29,1},{... | collective-permute-start | bytes 589832 | tf_op jit(solution)/shard_map/ppermute | solution.py:16
  26.1 35.6 %collective-permute-start.1 = (bf16[512,192]{0,1:T(8,128)(2,1)S(1)}, bf16[512,192]{0,1:T(8,128)(2,1)}, u32[]{:S(2)}, u32[]{:S(2)}) collective-permute-start(bf16[512,192]{0,1:T(8,128)(2,1)S(1)} %convolution_convert_fusion.19), channel_id=1, source_target_pairs={{24,0},{28,4},{0,8},{4,12},{8,16},{12,20},{16,24},{20,28},{25,1},{... | collective-permute-start | bytes 589832 | tf_op jit(solution)/shard_map/ppermute | solution.py:16
  70.9 150.6 %all-reduce.15.cloned.1.call-start = ((), (), s32[]{:S(2)}) async-start(), calls=%async_computation.8 | async-start | bytes 6291456 | tf_op jit(solution)/shard_map/psum | solution.py:138
  152.9 191.1 %all-reduce.17.cloned.1.call-start = ((), (), s32[]{:S(2)}) async-start(), calls=%async_computation.9 | async-start | bytes 6291456 | tf_op jit(solution)/shard_map/psum | solution.py:131
  232.3 35.3 %collective-permute-start.6 = (bf16[512,192]{0,1:T(8,128)(2,1)S(1)}, bf16[512,192]{0,1:T(8,128)(2,1)S(1)}, u32[]{:S(2)}, u32[]{:S(2)}) collective-permute-start(bf16[512,192]{0,1:T(8,128)(2,1)S(1)} %convolution_convert_fusion.18), channel_id=1, source_target_pairs={{28,0},{0,4},{4,8},{8,12},{12,16},{16,20},{20,24},{24,28},{29,1},{... | collective-permute-start | bytes 589832 | tf_op jit(solution)/shard_map/ppermute | solution.py:16
  278.8 154.9 %all-reduce.19.cloned.1.call-start = ((), (), s32[]{:S(2)}) async-start(), calls=%async_computation.10 | async-start | bytes 6291456 | tf_op jit(solution)/shard_map/psum | solution.py:193
  365.0 293.5 %all-reduce.21.cloned.1.call-start = ((), (), s32[]{:S(2)}) async-start(), calls=%async_computation.11 | async-start | bytes 6291456 | tf_op jit(solution)/shard_map/psum | solution.py:229
  514.0 48.6 %collective-permute-start.15 = (f32[512,192]{0,1:T(8,128)S(1)}, f32[512,192]{0,1:T(8,128)S(1)}, u32[]{:S(2)}, u32[]{:S(2)}) collective-permute-start(f32[512,192]{0,1:T(8,128)S(1)} %bitcast.497), channel_id=1, source_target_pairs={{4,0},{8,4},{12,8},{16,12},{20,16},{24,20},{28,24},{0,28},{5,1},{9... | collective-permute-start | bytes 1179656 | tf_op jit(solution)/shard_map/ppermute | solution.py:16
  518.3 44.4 %collective-permute-start.16 = (f32[512,192]{0,1:T(8,128)S(1)}, f32[512,192]{0,1:T(8,128)S(1)}, u32[]{:S(2)}, u32[]{:S(2)}) collective-permute-start(f32[512,192]{0,1:T(8,128)S(1)} %bitcast.495), channel_id=1, source_target_pairs={{8,0},{12,4},{16,8},{20,12},{24,16},{28,20},{0,24},{4,28},{9,1},{1... | collective-permute-start | bytes 1179656 | tf_op jit(solution)/shard_map/ppermute | solution.py:16
  520.2 41.4 %collective-permute-start.14 = (f32[512,192]{0,1:T(8,128)S(1)}, f32[512,192]{0,1:T(8,128)S(1)}, u32[]{:S(2)}, u32[]{:S(2)}) collective-permute-start(f32[512,192]{0,1:T(8,128)S(1)} %bitcast.498), channel_id=1, source_target_pairs={{12,0},{16,4},{20,8},{24,12},{28,16},{0,20},{4,24},{8,28},{13,1},{... | collective-permute-start | bytes 1179656 | tf_op jit(solution)/shard_map/ppermute | solution.py:16
  571.9 175.2 %all-reduce.23.cloned.1.call-start = ((), (), s32[]{:S(2)}) async-start(), calls=%async_computation.12 | async-start | bytes 6291456 | tf_op jit(solution)/shard_map/psum | solution.py:193
  678.4 340.1 %all-reduce.25.cloned.1.call-start = ((), (), s32[]{:S(2)}) async-start(), calls=%async_computation.20 | async-start | bytes 12582912 | tf_op jit(solution)/shard_map/psum | solution.py:138
  822.6 48.6 %collective-permute-start.21 = (f32[512,192]{0,1:T(8,128)S(1)}, f32[512,192]{0,1:T(8,128)S(1)}, u32[]{:S(2)}, u32[]{:S(2)}) collective-permute-start(f32[512,192]{0,1:T(8,128)S(1)} %bitcast.496), channel_id=1, source_target_pairs={{4,0},{8,4},{12,8},{16,12},{20,16},{24,20},{28,24},{0,28},{5,1},{9... | collective-permute-start | bytes 1179656 | tf_op jit(solution)/shard_map/ppermute | solution.py:16
  826.9 44.4 %collective-permute-start.22 = (f32[512,192]{0,1:T(8,128)S(1)}, f32[512,192]{0,1:T(8,128)S(1)}, u32[]{:S(2)}, u32[]{:S(2)}) collective-permute-start(f32[512,192]{0,1:T(8,128)S(1)} %bitcast.494), channel_id=1, source_target_pairs={{8,0},{12,4},{16,8},{20,12},{24,16},{28,20},{0,24},{4,28},{9,1},{1... | collective-permute-start | bytes 1179656 | tf_op jit(solution)/shard_map/ppermute | solution.py:16
  828.8 41.4 %collective-permute-start.20 = (f32[512,192]{0,1:T(8,128)S(1)}, f32[512,192]{0,1:T(8,128)S(1)}, u32[]{:S(2)}, u32[]{:S(2)}) collective-permute-start(f32[512,192]{0,1:T(8,128)S(1)} %bitcast.499), channel_id=1, source_target_pairs={{12,0},{16,4},{20,8},{24,12},{28,16},{0,20},{4,24},{8,28},{13,1},{... | collective-permute-start | bytes 1179656 | tf_op jit(solution)/shard_map/ppermute | solution.py:16
  880.5 204.7 %reduce-scatter.24.cloned.1.call-start = ((), (), s32[]{:S(2)}) async-start(), calls=%async_computation.17 | async-start | bytes 442368
  884.2 266.5 %reduce-scatter.28.cloned.1.call-start = ((), (), s32[]{:S(2)}) async-start(), calls=%async_computation.19 | async-start | bytes 1327104
  897.3 320.3 %reduce-scatter.26.cloned.1.call-start = ((), (), s32[]{:S(2)}) async-start(), calls=%async_computation.18 | async-start | bytes 1327104
  905.8 376.0 %reduce-scatter.22.cloned.1.call-start = ((), (), s32[]{:S(2)}) async-start(), calls=%async_computation.16 | async-start | bytes 442368
  1022.2 331.0 %reduce-scatter.16.cloned.1.call-start = ((), (), s32[]{:S(2)}) async-start(), calls=%async_computation.13 | async-start | bytes 2654208 | tf_op jit(solution)/shard_map/reduce_scatter | solution.py:327
  1025.6 608.2 %all-reduce.27.cloned.1.call-start = ((), (), s32[]{:S(2)}) async-start(), calls=%async_computation.21 | async-start | bytes 17301504
  1065.5 689.1 %reduce-scatter.20.cloned.1.call-start = ((), (), s32[]{:S(2)}) async-start(), calls=%async_computation.15 | async-start | bytes 7077888 | tf_op jit(solution)/shard_map/reduce_scatter | solution.py:342
  1074.3 801.3 %reduce-scatter.18.cloned.1.call-start = ((), (), s32[]{:S(2)}) async-start(), calls=%async_computation.14 | async-start | bytes 7077888 | tf_op jit(solution)/shard_map/reduce_scatter | solution.py:339
  (141 other events, 1577.6 us)
Sparse Core Ops, SparseCore 0:
  71.1 65.7 all-reduce.12
  153.0 68.5 all-reduce.14
  278.9 64.9 all-reduce.16
  365.1 68.5 all-reduce.18
  572.0 86.5 all-reduce.20
  678.5 68.5 all-reduce.22
  880.6 137.8 all-reduce.24
  1022.4 61.5 reduce-scatter.23
  1087.4 63.2 reduce-scatter.27
  1154.5 63.0 reduce-scatter.25
  1221.4 60.3 reduce-scatter.21
  1285.1 68.0 reduce-scatter.15
  1357.2 276.5 all-reduce.26
  1637.7 116.9 reduce-scatter.19
  1758.5 117.0 reduce-scatter.17
where the time goes:
time: 1890 us; the launch traced here: 1880 us
  waiting for transfers between devices  1400 us (74%)
  matrix products  249 us (13%)
  other arithmetic  89 us (5%)
  local copies, waits for them, and re-layouts  81.4 us (4%)
  starting transfers between devices  45.7 us (2%)
    unnamed x20, waiting for transfers between devices  462 us
    psum x2, waiting for transfers between devices, forward_layer(): result = middle + lax.psum(unit_part, 'tensor')  171 us
    psum x2, waiting for transfers between devices, backward_layer(): mlp_norm_grad = lax.psum(unit_back, 'tensor')  132 us
    psum x2, waiting for transfers between devices, forward_layer(): middle = residual_stream + lax.psum(head_part, 'tensor')  129 us
    reduce_scatter x1, waiting for transfers between devices, shards(): lax.psum_scatter(stacked[6].astype(jnp.bfloat16), 'dp', scatter_dimension...  119 us
    ppermute x24, waiting for transfers between devices, passed_along(): return lax.ppermute(block, axis, route)  118 us
    reduce_scatter x1, waiting for transfers between devices, shards(): lax.psum_scatter(stacked[7].astype(jnp.bfloat16), 'dp', scatter_dimension...  116 us
    psum x1, waiting for transfers between devices, backward_layer(): attn_norm_grad = lax.psum(head_back, 'tensor')  86.6 us
  transfers between devices with their start and end apart: 39, of which 25 were waited for; matrix products, arithmetic and copies ran while one was open for 9% of the time, Pallas kernels for 0%

commit v1 on v0

--- a/solution.py
+++ b/solution.py
@@ -8,6 +8,14 @@
 STRETCHES = 4
 EPS = 1e-05
 BASE = 100000.0
+
+
+def doubling_sum(array, mesh_axis):
+    size, summed = (lax.axis_size(mesh_axis), array)
+    for stride in [1 << k for k in range(size.bit_length() - 1)]:
+        route = [(i, i ^ stride) for i in range(size)]
+        summed = summed + lax.ppermute(summed, mesh_axis, route)
+    return summed
 
 
 def passed_along(block, axis, distance):
@@ -190,7 +198,7 @@
     unit_back = jnp.dot(gate_grad, gate_w.T, preferred_element_type=jnp.float32) + jnp.dot(
         up_grad, up_w.T, preferred_element_type=jnp.float32
     )
-    mlp_norm_grad = lax.psum(unit_back, "tensor")
+    mlp_norm_grad = doubling_sum(unit_back, "tensor")
     middle_grad, grad_gain_mlp = norm_back(middle, inv_mlp, gain_mlp, mlp_norm_grad, grad_flow)
     out_in = middle_grad.astype(jnp.bfloat16)
     grad_out = jnp.dot(mixed_heads.T, out_in, preferred_element_type=jnp.float32)

time: 1890 us -> 1900 us (level)
    ppermute x0 -> x4, waiting for transfers between devices: none -> 147 us  [doubling_sum(): summed = summed + lax.ppermute(summed, mesh_axis, route)]
    psum x2 -> x0, waiting for transfers between devices: 132 us -> none  [backward_layer(): mlp_norm_grad = lax.psum(unit_back, 'tensor')]
    unnamed x269 -> x257, local copies, waits for them, and re-layouts: 43.1 us -> 44.5 us
    unnamed x20 -> x18, waiting for transfers between devices: 462 us -> 461 us
  transfers between devices with their start and end apart: 39 -> 41, of which waited for: 25 -> 27; matrix products, arithmetic and copies ran while one was open for 9% -> 8% of each run, Pallas kernels for 0% -> 0%
where the time goes in v1:
time: 1900 us; the launch traced here: 1890 us
  waiting for transfers between devices  1410 us (74%)
  matrix products  247 us (13%)
  local copies, waits for them, and re-layouts  83.8 us (4%)
  other arithmetic  81.1 us (4%)
  starting transfers between devices  46.8 us (2%)
    unnamed x18, waiting for transfers between devices  461 us
    psum x2, waiting for transfers between devices, forward_layer(): result = middle + lax.psum(unit_part, 'tensor')  171 us
    ppermute x4, waiting for transfers between devices, doubling_sum(): summed = summed + lax.ppermute(summed, mesh_axis, route)  147 us
    psum x2, waiting for transfers between devices, forward_layer(): middle = residual_stream + lax.psum(head_part, 'tensor')  129 us
    reduce_scatter x1, waiting for transfers between devices, shards(): lax.psum_scatter(stacked[7].astype(jnp.bfloat16), 'dp', scatter_dimension...  119 us
    reduce_scatter x1, waiting for transfers between devices, shards(): lax.psum_scatter(stacked[6].astype(jnp.bfloat16), 'dp', scatter_dimension...  118 us
    ppermute x24, waiting for transfers between devices, passed_along(): return lax.ppermute(block, axis, route)  113 us
    psum x1, waiting for transfers between devices, backward_layer(): attn_norm_grad = lax.psum(head_back, 'tensor')  86.4 us
  transfers between devices with their start and end apart: 41, of which 27 were waited for; matrix products, arithmetic and copies ran while one was open for 8% of the time, Pallas kernels for 0%

profile of v1, /device:TPU:0, one launch (start us, length us, event | category | flops | bytes accessed | tf_op | source)
XLA Modules:
  0.0 1890.3 jit_solution(13806280222664640690)
XLA Ops:
  42.1 11.3 collective-permute-done.5
  74.9 63.9 %all-reduce.11.cloned.1.call-done = f32[512,1536]{1,0:T(8,128)} async-done(((f32[512,1536]{1,0:T(8,128)}), f32[512,1536]{1,0:T(8,128)}) %all-reduce.11.cloned.1.call-update) | async-done | bytes 3145744 | tf_op jit(solution)/shard_map/psum | solution.py:139
  157.7 66.0 %all-reduce.13.cloned.1.call-done = f32[512,1536]{1,0:T(8,128)} async-done(((f32[512,1536]{1,0:T(8,128)}), f32[512,1536]{1,0:T(8,128)}) %all-reduce.13.cloned.1.call-update) | async-done | bytes 3145744 | tf_op jit(solution)/shard_map/psum | solution.py:146
  240.6 22.9 %collective-permute-done.11 = bf16[512,192]{0,1:T(8,128)(2,1)S(1)} collective-permute-done((bf16[512,192]{0,1:T(8,128)(2,1)S(1)}, bf16[512,192]{0,1:T(8,128)(2,1)S(1)}, u32[]{:S(2)}, u32[]{:S(2)}) %collective-permute-start.11) | collective-permute-done | bytes 196640 | tf_op jit(solution)/shard_map/ppermute | solution.py:24
  281.7 64.9 %all-reduce.15.cloned.1.call-done = f32[512,1536]{1,0:T(8,128)} async-done(((f32[512,1536]{1,0:T(8,128)}), f32[512,1536]{1,0:T(8,128)}) %all-reduce.15.cloned.1.call-update) | async-done | bytes 3145744 | tf_op jit(solution)/shard_map/psum | solution.py:139
  373.2 69.7 %collective-permute-done.13 = f32[512,1536]{1,0:T(8,128)S(1)} collective-permute-done((f32[512,1536]{1,0:T(8,128)S(1)}, f32[512,1536]{1,0:T(8,128)S(1)}, u32[]{:S(2)}, u32[]{:S(2)}) %collective-permute-start.13) | collective-permute-done | bytes 3145760 | tf_op jit(solution)/shard_map/ppermute | solution.py:17
  448.3 9.5 convolution_bitcast_fusion.1
  466.1 25.2 %fusion.63 = f32[2048,2,96]{0,2,1:T(8,128)} fusion(bf16[512,2,2,96]{0,3,2,1:T(8,128)(2,1)} %bitcast.491, f32[2,2048,512,2]{2,1,3,0:T(8,128)} %fusion.188, f32[2,2048,512,2]{2,1,3,0:T(8,128)} %copy-done.11, f32[2,2,512]{2,1,0:T(2,128)S(1)} %copy-done.87, pred[512,2048]{0,1:T(8,128)(4,1)} %copy-done.21), kind=kOutput, calls=%fused_computation.113 | convolution fusion | flops 851447808 | bytes 36577280 | tf_op jit(solution)/shard_map/kgqt,qkgd->tkd/dot_general | solution.py:91
  491.3 25.1 %fusion.41 = f32[2,96,2,512]{3,1,2,0:T(8,128)} fusion(f32[2,2048,512,2]{2,1,3,0:T(8,128)} %fusion.188, f32[2,2048,512,2]{2,1,3,0:T(8,128)} %copy-done.11, f32[2,2,512]{2,1,0:T(2,128)S(1)} %copy-done.87, pred[512,2048]{0,1:T(8,128)(4,1)} %copy-done.21, bf16[512,2,96]{0,2,1:T(8,128)(2,1)} %bitcast.530, bf16[512,2,96]{0,2,1:T(8,128)(2,1)} %bitcast.528, ...), kind=kOutput, calls=%fused_computation.87 | convolution fusion | flops 854593536 | bytes 36184064 | tf_op jit(solution)/shard_map/kgqt,tkd->qkgd/dot_general | solution.py:88
  529.8 19.0 %collective-permute-done.14 = f32[512,192]{0,1:T(8,128)S(1)} collective-permute-done((f32[512,192]{0,1:T(8,128)S(1)}, f32[512,192]{0,1:T(8,128)S(1)}, u32[]{:S(2)}, u32[]{:S(2)}) %collective-permute-start.14) | collective-permute-done | bytes 393248 | tf_op jit(solution)/shard_map/ppermute | solution.py:24
  575.5 86.4 %all-reduce.17.cloned.1.call-done = f32[512,1536]{1,0:T(8,128)} async-done(((f32[512,1536]{1,0:T(8,128)}), f32[512,1536]{1,0:T(8,128)}) %all-reduce.17.cloned.1.call-update) | async-done | bytes 3145744 | tf_op jit(solution)/shard_map/psum | solution.py:237
  687.8 66.2 %collective-permute-done.21 = f32[512,1536]{1,0:T(8,128)S(1)} collective-permute-done((f32[512,1536]{1,0:T(8,128)S(1)}, f32[512,1536]{1,0:T(8,128)S(1)}, u32[]{:S(2)}, u32[]{:S(2)}) %collective-permute-start.21) | collective-permute-done | bytes 3145760 | tf_op jit(solution)/shard_map/ppermute | solution.py:17
  776.5 24.6 %fusion.62 = f32[2048,2,96]{0,2,1:T(8,128)} fusion(bf16[512,2,2,96]{0,3,2,1:T(8,128)(2,1)S(1)} %bitcast.489, f32[2,2048,512,2]{2,1,3,0:T(8,128)} %fusion.189, f32[2,2048,512,2]{2,1,3,0:T(8,128)} %copy-done.10, f32[2,2,512]{2,1,0:T(2,128)S(1)} %copy-done.85, pred[512,2048]{0,1:T(8,128)(4,1)S(1)} %copy-done.24), kind=kOutput, calls=%fused_computation.112 | convolution fusion | flops 851447808 | bytes 36577280 | tf_op jit(solution)/shard_map/kgqt,qkgd->tkd/dot_general | solution.py:91
  801.2 23.6 %fusion.44 = f32[2,96,2,512]{3,1,2,0:T(8,128)S(1)} fusion(f32[2,2048,512,2]{2,1,3,0:T(8,128)} %fusion.189, f32[2,2048,512,2]{2,1,3,0:T(8,128)} %copy-done.10, f32[2,2,512]{2,1,0:T(2,128)S(1)} %copy-done.85, pred[512,2048]{0,1:T(8,128)(4,1)S(1)} %copy-done.24, bf16[512,2,96]{0,2,1:T(8,128)(2,1)} %bitcast.14, bf16[512,2,96]{0,2,1:T(8,128)(2,1)} %bitcast.13, ...), kind=kOutput, calls=%fused_computation.90 | convolution fusion | flops 854593536 | bytes 36184064 | tf_op jit(solution)/shard_map/kgqt,tkd->qkgd/dot_general | solution.py:88
  838.4 19.0 %collective-permute-done.22 = f32[512,192]{0,1:T(8,128)S(1)} collective-permute-done((f32[512,192]{0,1:T(8,128)S(1)}, f32[512,192]{0,1:T(8,128)S(1)}, u32[]{:S(2)}, u32[]{:S(2)}) %collective-permute-start.22) | collective-permute-done | bytes 393248 | tf_op jit(solution)/shard_map/ppermute | solution.py:24
  917.0 104.9 %all-reduce.19.cloned.1.call-done = (f32[512,1536]{1,0:T(8,128)}, f32[512,1536]{1,0:T(8,128)}) async-done(((f32[512,1536]{1,0:T(8,128)}, f32[512,1536]{1,0:T(8,128)}), (f32[512,1536]{1,0:T(8,128)}, f32[512,1536]{1,0:T(8,128)})) %all-reduce.19.cloned.1.call-update) | async-done | bytes 6291472 | tf_op jit(solution)/shard_map/psum | solution.py:146
  1059.2 16.4 copy.64
  1090.2 63.6 %reduce-scatter.28.cloned.1.call-done = bf16[192,384]{1,0:T(8,128)(2,1)} async-done(((bf16[1536,384]{1,0:T(8,128)(2,1)}), bf16[192,384]{1,0:T(8,128)(2,1)}) %reduce-scatter.28.cloned.1.call-update) | async-done | bytes 147472
  1155.9 64.9 %reduce-scatter.26.cloned.1.call-done = bf16[192,384]{1,0:T(8,128)(2,1)} async-done(((bf16[1536,384]{1,0:T(8,128)(2,1)}), bf16[192,384]{1,0:T(8,128)(2,1)}) %reduce-scatter.26.cloned.1.call-update) | async-done | bytes 147472
  1230.7 54.4 %reduce-scatter.22.cloned.1.call-done = bf16[192,2]{1,0:T(8,128)(2,1)} async-done(((bf16[1536,2]{1,0:T(8,128)(2,1)}), bf16[192,2]{1,0:T(8,128)(2,1)}) %reduce-scatter.22.cloned.1.call-update) | async-done | bytes 784
  1286.5 69.9 %reduce-scatter.16.cloned.1.call-done = bf16[2,192,384]{2,1,0:T(8,128)(2,1)} async-done(((bf16[2,1536,384]{2,1,0:T(8,128)(2,1)}), bf16[2,192,384]{2,1,0:T(8,128)(2,1)}) %reduce-scatter.16.cloned.1.call-update) | async-done | bytes 294928 | tf_op jit(solution)/shard_map/reduce_scatter | solution.py:335
  1358.2 118.9 %reduce-scatter.20.cloned.1.call-done = bf16[2,192,1024]{2,1,0:T(8,128)(2,1)} async-done(((bf16[2,1536,1024]{2,1,0:T(8,128)(2,1)}), bf16[2,192,1024]{2,1,0:T(8,128)(2,1)}) %reduce-scatter.20.cloned.1.call-update) | async-done | bytes 786448 | tf_op jit(solution)/shard_map/reduce_scatter | solution.py:350
  1479.5 118.1 %reduce-scatter.18.cloned.1.call-done = bf16[2,192,1024]{2,1,0:T(8,128)(2,1)} async-done(((bf16[2,1536,1024]{2,1,0:T(8,128)(2,1)}), bf16[2,192,1024]{2,1,0:T(8,128)(2,1)}) %reduce-scatter.18.cloned.1.call-update) | async-done | bytes 786448 | tf_op jit(solution)/shard_map/reduce_scatter | solution.py:347
  1600.1 278.1 %all-reduce.21.cloned.1.call-done = (bf16[2,384,1536]{1,0,2:T(2,128)(2,1)}, bf16[2,1024,1536]{1,0,2:T(2,128)(2,1)}) async-done(((bf16[2,384,1536]{1,0,2:T(2,128)(2,1)}, bf16[2,1024,1536]{1,0,2:T(2,128)(2,1)}), (bf16[2,384,1536]{1,0,2:T(2,128)(2,1)}, bf16[2,1024,1536]{1,0,2:T(2,128)(2,1)})) %all-reduce.21.cloned.1.call-update) | async-done | bytes 8650768
  (495 shorter events, 387.1 us)
Async XLA Ops:
  7.2 131.7 %all-reduce.11.cloned.1.call-start = ((), (), s32[]{:S(2)}) async-start(), calls=%async_computation.7 | async-start | bytes 6291456 | tf_op jit(solution)/shard_map/psum | solution.py:139
  25.2 36.5 %collective-permute-start = (bf16[512,192]{0,1:T(8,128)(2,1)}, bf16[512,192]{0,1:T(8,128)(2,1)}, u32[]{:S(2)}, u32[]{:S(2)}) collective-permute-start(bf16[512,192]{0,1:T(8,128)(2,1)} %convolution_convert_fusion.19), channel_id=1, source_target_pairs={{28,0},{0,4},{4,8},{8,12},{12,16},{16,20},{20,24},{24,28},{29,1},{... | collective-permute-start | bytes 589832 | tf_op jit(solution)/shard_map/ppermute | solution.py:24
  26.7 35.0 %collective-permute-start.1 = (bf16[512,192]{0,1:T(8,128)(2,1)}, bf16[512,192]{0,1:T(8,128)(2,1)}, u32[]{:S(2)}, u32[]{:S(2)}) collective-permute-start(bf16[512,192]{0,1:T(8,128)(2,1)} %convolution_convert_fusion.19), channel_id=1, source_target_pairs={{24,0},{28,4},{0,8},{4,12},{8,16},{12,20},{16,24},{20,28},{25,1},{... | collective-permute-start | bytes 589832 | tf_op jit(solution)/shard_map/ppermute | solution.py:24
  73.0 150.7 %all-reduce.13.cloned.1.call-start = ((), (), s32[]{:S(2)}) async-start(), calls=%async_computation.8 | async-start | bytes 6291456 | tf_op jit(solution)/shard_map/psum | solution.py:146
  155.0 191.6 %all-reduce.15.cloned.1.call-start = ((), (), s32[]{:S(2)}) async-start(), calls=%async_computation.9 | async-start | bytes 6291456 | tf_op jit(solution)/shard_map/psum | solution.py:139
  235.0 35.3 %collective-permute-start.6 = (bf16[512,192]{0,1:T(8,128)(2,1)S(1)}, bf16[512,192]{0,1:T(8,128)(2,1)S(1)}, u32[]{:S(2)}, u32[]{:S(2)}) collective-permute-start(bf16[512,192]{0,1:T(8,128)(2,1)S(1)} %convolution_convert_fusion.18), channel_id=1, source_target_pairs={{28,0},{0,4},{4,8},{8,12},{12,16},{16,20},{20,24},{24,28},{29,1},{... | collective-permute-start | bytes 589832 | tf_op jit(solution)/shard_map/ppermute | solution.py:24
  281.5 380.4 %all-reduce.17.cloned.1.call-start = ((), (), s32[]{:S(2)}) async-start(), calls=%async_computation.10 | async-start | bytes 6291456 | tf_op jit(solution)/shard_map/psum | solution.py:237
  372.7 70.2 %collective-permute-start.13 = (f32[512,1536]{1,0:T(8,128)S(1)}, f32[512,1536]{1,0:T(8,128)S(1)}, u32[]{:S(2)}, u32[]{:S(2)}) collective-permute-start(f32[512,1536]{1,0:T(8,128)S(1)} %add.317), channel_id=1, source_target_pairs={{0,2},{1,3},{2,0},{3,1},{4,6},{5,7},{6,4},{7,5},{8,10},{9,11},{10,... | collective-permute-start | bytes 9437192 | tf_op jit(solution)/shard_map/ppermute | solution.py:17
  518.1 48.7 %collective-permute-start.17 = (f32[512,192]{0,1:T(8,128)S(1)}, f32[512,192]{0,1:T(8,128)S(1)}, u32[]{:S(2)}, u32[]{:S(2)}) collective-permute-start(f32[512,192]{0,1:T(8,128)S(1)} %bitcast.497), channel_id=1, source_target_pairs={{4,0},{8,4},{12,8},{16,12},{20,16},{24,20},{28,24},{0,28},{5,1},{9... | collective-permute-start | bytes 1179656 | tf_op jit(solution)/shard_map/ppermute | solution.py:24
  522.3 44.4 %collective-permute-start.18 = (f32[512,192]{0,1:T(8,128)S(1)}, f32[512,192]{0,1:T(8,128)S(1)}, u32[]{:S(2)}, u32[]{:S(2)}) collective-permute-start(f32[512,192]{0,1:T(8,128)S(1)} %bitcast.495), channel_id=1, source_target_pairs={{8,0},{12,4},{16,8},{20,12},{24,16},{28,20},{0,24},{4,28},{9,1},{1... | collective-permute-start | bytes 1179656 | tf_op jit(solution)/shard_map/ppermute | solution.py:24
  524.2 41.5 %collective-permute-start.16 = (f32[512,192]{0,1:T(8,128)S(1)}, f32[512,192]{0,1:T(8,128)S(1)}, u32[]{:S(2)}, u32[]{:S(2)}) collective-permute-start(f32[512,192]{0,1:T(8,128)S(1)} %bitcast.498), channel_id=1, source_target_pairs={{12,0},{16,4},{20,8},{24,12},{28,16},{0,20},{4,24},{8,28},{13,1},{... | collective-permute-start | bytes 1179656 | tf_op jit(solution)/shard_map/ppermute | solution.py:24
  575.5 446.4 %all-reduce.19.cloned.1.call-start = ((), (), s32[]{:S(2)}) async-start(), calls=%async_computation.18 | async-start | bytes 12582912 | tf_op jit(solution)/shard_map/psum | solution.py:146
  683.8 70.2 %collective-permute-start.21 = (f32[512,1536]{1,0:T(8,128)S(1)}, f32[512,1536]{1,0:T(8,128)S(1)}, u32[]{:S(2)}, u32[]{:S(2)}) collective-permute-start(f32[512,1536]{1,0:T(8,128)S(1)} %add.333), channel_id=1, source_target_pairs={{0,2},{1,3},{2,0},{3,1},{4,6},{5,7},{6,4},{7,5},{8,10},{9,11},{10,... | collective-permute-start | bytes 9437192 | tf_op jit(solution)/shard_map/ppermute | solution.py:17
  826.6 48.7 %collective-permute-start.25 = (f32[512,192]{0,1:T(8,128)S(1)}, f32[512,192]{0,1:T(8,128)S(1)}, u32[]{:S(2)}, u32[]{:S(2)}) collective-permute-start(f32[512,192]{0,1:T(8,128)S(1)} %bitcast.496), channel_id=1, source_target_pairs={{4,0},{8,4},{12,8},{16,12},{20,16},{24,20},{28,24},{0,28},{5,1},{9... | collective-permute-start | bytes 1179656 | tf_op jit(solution)/shard_map/ppermute | solution.py:24
  830.9 44.4 %collective-permute-start.26 = (f32[512,192]{0,1:T(8,128)S(1)}, f32[512,192]{0,1:T(8,128)S(1)}, u32[]{:S(2)}, u32[]{:S(2)}) collective-permute-start(f32[512,192]{0,1:T(8,128)S(1)} %bitcast.494), channel_id=1, source_target_pairs={{8,0},{12,4},{16,8},{20,12},{24,16},{28,20},{0,24},{4,28},{9,1},{1... | collective-permute-start | bytes 1179656 | tf_op jit(solution)/shard_map/ppermute | solution.py:24
  832.8 41.5 %collective-permute-start.24 = (f32[512,192]{0,1:T(8,128)S(1)}, f32[512,192]{0,1:T(8,128)S(1)}, u32[]{:S(2)}, u32[]{:S(2)}) collective-permute-start(f32[512,192]{0,1:T(8,128)S(1)} %bitcast.499), channel_id=1, source_target_pairs={{12,0},{16,4},{20,8},{24,12},{28,16},{0,20},{4,24},{8,28},{13,1},{... | collective-permute-start | bytes 1179656 | tf_op jit(solution)/shard_map/ppermute | solution.py:24
  884.1 204.6 %reduce-scatter.24.cloned.1.call-start = ((), (), s32[]{:S(2)}) async-start(), calls=%async_computation.15 | async-start | bytes 442368
  887.8 266.0 %reduce-scatter.28.cloned.1.call-start = ((), (), s32[]{:S(2)}) async-start(), calls=%async_computation.17 | async-start | bytes 1327104
  900.9 319.9 %reduce-scatter.26.cloned.1.call-start = ((), (), s32[]{:S(2)}) async-start(), calls=%async_computation.16 | async-start | bytes 1327104
  909.4 375.6 %reduce-scatter.22.cloned.1.call-start = ((), (), s32[]{:S(2)}) async-start(), calls=%async_computation.14 | async-start | bytes 442368
  1025.6 330.8 %reduce-scatter.16.cloned.1.call-start = ((), (), s32[]{:S(2)}) async-start(), calls=%async_computation.11 | async-start | bytes 2654208 | tf_op jit(solution)/shard_map/reduce_scatter | solution.py:335
  1029.0 448.1 %reduce-scatter.20.cloned.1.call-start = ((), (), s32[]{:S(2)}) async-start(), calls=%async_computation.13 | async-start | bytes 7077888 | tf_op jit(solution)/shard_map/reduce_scatter | solution.py:350
  1038.1 559.5 %reduce-scatter.18.cloned.1.call-start = ((), (), s32[]{:S(2)}) async-start(), calls=%async_computation.12 | async-start | bytes 7077888 | tf_op jit(solution)/shard_map/reduce_scatter | solution.py:347
  1047.0 831.2 %all-reduce.21.cloned.1.call-start = ((), (), s32[]{:S(2)}) async-start(), calls=%async_computation.19 | async-start | bytes 17301504
  (137 other events, 2062.6 us)
Sparse Core Ops, SparseCore 0:
  73.1 65.7 all-reduce.10
  155.1 68.5 all-reduce.12
  281.6 64.9 all-reduce.14
  575.6 86.2 all-reduce.16
  884.2 137.6 all-reduce.18
  1025.6 61.5 reduce-scatter.23
  1090.5 63.2 reduce-scatter.27
  1157.8 62.9 reduce-scatter.25
  1224.7 60.3 reduce-scatter.21
  1288.4 68.0 reduce-scatter.15
  1360.0 117.0 reduce-scatter.19
  1480.5 117.0 reduce-scatter.17
  1601.7 276.5 all-reduce.20
